TPU v7x, 256 devices: a whole 4x4x8 slice. The times are simulated.
256 devices in a mesh: dp: 64 (over z, x, core), section: 4 (over y).
Axes of the slice: x: 4, y: 4, z: 8, core: 2. Of those that a mesh axis runs over, the one named last changes fastest.
Arguments:
- token_ids: int32 [4, 64, 128], P('section', 'dp'), may hold values from 0 to 511
- segment_ids: int32 [4, 64, 128], P('section', 'dp'), may hold values from 0 to 3, never falling along the last dimension, each value on 1 to 64 neighbouring positions
- row_order: int32 [4, 64], P('section', 'dp'), may hold values from 0 to 63, each once within a row
- embed_table: bfloat16 [4, 512, 4096], P('section'), may hold values from -6 to 6
- norm_gain: float32 [4, 4096], P('section'), may hold values from 0.5 to 2
- position_bias: float32 [4, 32, 64], P('section'), may hold values from -4 to 4
- returned_grad: bfloat16 [4, 8192, 4096], P('section', 'dp'), may hold values from -6 to 6
Outputs:
- handed: bfloat16 [4, 8192, 4096], P('section', 'dp')
- grad_table: float32 [4, 512, 4096], P('section', 'dp')
- grad_gain: float32 [4, 4096], P('section')
- grad_bias: float32 [4, 32, 64], P('section')
All inputs are finite; a program needn't handle non-finite values.
Results may differ from a plain program's by a relative error of at most 0.014.
Values may be sent and summed in bfloat16 or wider, within the bound.
No kernel may reach another device: no remote copies, remote signals or barrier semaphores. Data moves between devices by JAX's collectives and lax.ppermute only.
A program may use at most 128 MiB of HBM per device.

v0:
```python
import jax
import jax.numpy as jnp
from jax import lax
from jax.sharding import PartitionSpec as P

limits = (12, 16, 23, 32, 45, 64, 91)


def passed_along(value, axis, steps):
    count = lax.axis_size(axis)
    pairs = [(source, (source + steps) % count) for source in range(count)]
    return lax.ppermute(value, axis, pairs)


def bucket_table(length):
    places = jnp.arange(length, dtype=jnp.int32)
    offset = places[None, :] - places[:, None]
    apart = jnp.abs(offset)
    bucket = jnp.minimum(apart, 8)
    for limit in limits:
        bucket = bucket + (apart >= limit).astype(jnp.int32)
    bucket = bucket + 16 * (offset > 0).astype(jnp.int32)
    return bucket


def attend_row(row_normed, row_segs, bias_full, heads, head_size):
    length = row_normed.shape[0]
    split = row_normed.reshape(length, heads, head_size).astype(jnp.float32)
    scores = jnp.einsum("qhd,khd->hqk", split, split) / head_size + bias_full
    same = row_segs[:, None] == row_segs[None, :]
    scores = jnp.where(same[None, :, :], scores, -1e30)
    top = jnp.max(scores, axis=-1, keepdims=True)
    expo = jnp.exp(scores - top)
    probs = (expo / jnp.sum(expo, axis=-1, keepdims=True)).astype(jnp.bfloat16)
    mixed = jnp.einsum("hqk,khd->qhd", probs.astype(jnp.float32), split)
    return mixed.reshape(length, heads * head_size)


def layer(embedded, gain, bias, segs):
    rows_count, length = segs.shape
    width = embedded.shape[1]
    heads = bias.shape[1]
    head_size = width // heads
    wide = embedded.astype(jnp.float32)
    meansq = jnp.mean(wide * wide, axis=-1, keepdims=True)
    normed = (wide * lax.rsqrt(meansq + 1e-06) * gain).astype(jnp.bfloat16)
    picks = (bucket_table(length)[:, :, None] == jnp.arange(bias.shape[0], dtype=jnp.int32)).astype(
        jnp.float32
    )
    bias_full = jnp.einsum("qkb,bh->hqk", picks, bias)
    blocks = normed.reshape(rows_count, length, width)
    mixed = jax.vmap(
        lambda row_block, row_segs: attend_row(row_block, row_segs, bias_full, heads, head_size)
    )(blocks, segs)
    return (wide + mixed.reshape(rows_count * length, width)).astype(jnp.bfloat16)


def local(token_ids, segment_ids, row_order, embed_table, norm_gain, position_bias, returned_grad):
    all_ids, all_segs = (
        lax.all_gather(token_ids[0], "dp", axis=0, tiled=True),
        lax.all_gather(segment_ids[0], "dp", axis=0, tiled=True),
    )
    order = row_order[0]
    packed = jnp.take(all_ids, order, axis=0)
    row_segs = jnp.take(all_segs, order, axis=0)
    vocab = embed_table.shape[1]
    onehot = (packed.reshape(-1)[:, None] == jnp.arange(vocab, dtype=jnp.int32)[None, :]).astype(
        jnp.bfloat16
    )
    embedded = jnp.dot(onehot, embed_table[0], preferred_element_type=jnp.float32).astype(
        jnp.bfloat16
    )
    result, pullback = jax.vjp(
        lambda first, second, third: layer(first, second, third, row_segs),
        embedded,
        norm_gain[0],
        position_bias[0],
    )
    handed = passed_along(result, "section", 1)
    incoming = passed_along(returned_grad[0], "section", -1)
    grad_rows, grad_g, grad_b = pullback(incoming)
    table_term = lax.dot_general(
        onehot, grad_rows, (((0,), (0,)), ((), ())), preferred_element_type=jnp.float32
    )
    grad_tab = lax.psum_scatter(table_term, "dp", scatter_dimension=0, tiled=True)
    grad_g, grad_b = lax.psum((grad_g, grad_b), "dp")
    return (handed[None], grad_tab[None], grad_g[None], grad_b[None])


def solution(mesh):
    placed = (
        P("section", "dp", None),
        P("section", "dp", None),
        P("section", "dp"),
        P("section", None, None),
        P("section", None),
        P("section", None, None),
        P("section", "dp", None),
    )
    return jax.shard_map(
        local,
        mesh=mesh,
        in_specs=placed,
        out_specs=(
            P("section", "dp", None),
            P("section", "dp", None),
            P("section", None),
            P("section", None, None),
        ),
        check_vma=False,
    )
```

profile of v0, /device:TPU:24, one launch (start us, length us, event | category | flops | bytes accessed | tf_op | source)
XLA Modules:
  0.0 409.5 jit_solution(6703125069498743781)
XLA Ops:
  7.2 0.0 copy-start
  7.2 0.0 copy-start.8
  7.2 0.0 all-reduce.4.cloned.1.call-start
  7.2 0.8 collective-permute-start.1
  8.1 0.1 select_add_fusion
  8.8 42.7 %all-gather = s32[64,1,128]{2,1,0:T(1,128)S(1)} all-gather(s32[1,1,128]{2,1,0:T(1,128)} %param.9), channel_id=2, replica_groups=mesh['dp'=64,'section'=4] {'dp'}, dimensions={0}, use_global_device_ids=true | all-gather | bytes 33280 | tf_op jit(solution)/shard_map/all_gather | solution.py:60
  51.5 0.0 copy-start.7
  51.5 3.0 multiply_reduce_fusion.2
  54.5 0.0 copy-done.8
  54.5 37.3 %all-gather.1 = s32[64,1,128]{2,1,0:T(1,128)S(1)} all-gather(s32[1,1,128]{2,1,0:T(1,128)S(1)} %copy-done.8), channel_id=3, replica_groups=mesh['dp'=64,'section'=4] {'dp'}, dimensions={0}, use_global_device_ids=true | all-gather | bytes 33280 | tf_op jit(solution)/shard_map/all_gather | solution.py:61
  91.9 0.0 copy-done
  91.9 2.7 fusion.17
  94.6 0.0 copy-done.7
  94.6 1.2 multiply_convert_fusion
  95.8 0.1 broadcast_compare_fusion.1
  95.9 1.6 copy.37
  97.5 5.4 %copy.38 = f32[128,128,64]{0,1,2:T(8,128)} copy(f32[128,128,64]{1,2,0:T(8,128)} %fusion.17) | data formatting | bytes 8388608 | tf_op jit(solution)/shard_map/jvp(qkb,bh->hqk)/dot_general | solution.py:50
  102.9 3.3 fusion.47
  106.2 0.0 copy-start.2
  106.2 1.9 copy-done.2
  108.1 0.9 fusion.13
  109.1 0.0 collective-permute-done.1
  109.1 2.3 copy.41
  111.4 0.0 copy-start.3
  111.4 4.1 fusion.6
  115.4 0.0 copy-done.3
  115.5 2.6 convert_reduce_fusion
  118.0 2.2 add_select_fusion
  120.2 0.0 copy-start.4
  120.2 1.5 fusion.11
  121.8 0.7 fusion.9
  122.4 0.0 copy-done.4
  122.4 0.0 copy-start.6
  122.5 2.0 fusion.50
  124.4 0.0 copy-done.6
  124.4 1.5 fusion.15
  126.0 1.5 bitcast_convert_fusion
  127.5 2.9 copy.45
  130.4 2.9 copy.40
  133.3 0.0 copy-start.5
  133.3 4.0 multiply_reduce_fusion
  137.4 0.0 copy-done.5
  137.4 5.9 %fusion.21 = f32[512,4096]{1,0:T(8,128)} fusion(f32[128,4096]{1,0:T(8,128)S(1)} %get-tuple-element.27, bf16[128,4096]{1,0:T(8,128)(2,1)} %collective-permute-done.1, f32[128,4096]{1,0:T(8,128)S(1)} %copy-done.5, f32[128]{0:T(128)S(1)} %multiply_multiply_fusion, f32[4096]{0:T(1024)S(1)} %bitcast.114, f32[128]{0:T(128)S(1)} %fusion.42, s32[128]{0:T(128)S(1)} %fusion.40), kind=kOutput, calls=%fused_computation.40 | convolution fusion | flops 541130752 | bytes 13649408 | tf_op jit(solution)/shard_map/dot_general | solution.py:82
  143.3 0.0 copy-start.9
  143.3 0.0 all-reduce.4.cloned.1.call-update
  143.3 2.6 collective-permute-start
  145.9 0.0 copy-done.9
  145.9 0.6 dynamic-slice.7
  146.4 0.0 copy-start.1
  147.1 4.1 copy.47
  151.2 0.7 fusion.20
  151.9 248.2 %all-reduce.1 = (f32[1,4096]{1,0:T(1,128)}, f32[1,32,64]{2,1,0:T(8,128)}) all-reduce(f32[1,4096]{1,0:T(1,128)S(1)} %bitcast.115, f32[1,32,64]{2,1,0:T(8,128)S(1)} %fusion.20), channel_id=1, replica_groups=mesh['dp'=64,'section'=4] {'dp'}, use_global_device_ids=true, to_apply=%region_9.11 | all-reduce | flops 6144 | bytes 49152 | tf_op jit(solution)/shard_map/psum | solution.py:86
  400.1 0.0 collective-permute-done
  400.1 0.0 all-reduce.4.cloned.1.call-done
  400.1 1.6 dynamic-slice_bitcast_fusion
  401.7 1.0 copy.55
  402.6 0.0 copy-done.1
  (7 shorter events, 0.1 us)
Async XLA Ops:
  7.2 84.7 %copy-start = (f32[1,32,64]{2,1,0:T(8,128)S(1)}, f32[1,32,64]{2,1,0:T(8,128)}, u32[]{:S(2)}) copy-start(f32[1,32,64]{2,1,0:T(8,128)} %param.14) | copy-start | bytes 24580
  7.2 47.3 %copy-start.8 = (s32[1,1,128]{2,1,0:T(1,128)S(1)}, s32[1,1,128]{2,1,0:T(1,128)}, u32[]{:S(2)}) copy-start(s32[1,1,128]{2,1,0:T(1,128)} %param.10) | copy-start | bytes 1540
  7.2 392.9 %all-reduce.4.cloned.1.call-start = ((), (), s32[]{:S(2)}) async-start(), calls=%async_computation | async-start | bytes 16777216
  7.2 101.9 %collective-permute-start.1 = (bf16[128,4096]{1,0:T(8,128)(2,1)}, bf16[128,4096]{1,0:T(8,128)(2,1)}, u32[]{:S(2)}, u32[]{:S(2)}) collective-permute-start(bf16[128,4096]{1,0:T(8,128)(2,1)} %bitcast.118), channel_id=1, source_target_pairs={{0,3},{1,0},{2,1},{3,2},{4,7},{5,4},{6,5},{7,6},{8,11},{9,8},{10,9... | collective-permute-start | bytes 3145736 | tf_op jit(solution)/shard_map/ppermute | solution.py:12
  51.5 43.1 %copy-start.7 = (f32[1,4096]{1,0:T(1,128)S(1)}, f32[1,4096]{1,0:T(1,128)}, u32[]{:S(2)}) copy-start(f32[1,4096]{1,0:T(1,128)} %param.13) | copy-start | bytes 49156
  106.2 1.9 copy-start.2
  111.4 4.1 copy-start.3
  120.2 2.2 copy-start.4
  122.4 2.0 copy-start.6
  133.3 4.0 copy-start.5
  143.3 2.6 copy-start.9
  143.3 256.8 %collective-permute-start = (bf16[128,4096]{1,0:T(8,128)(2,1)}, bf16[128,4096]{1,0:T(8,128)(2,1)S(1)}, u32[]{:S(2)}, u32[]{:S(2)}) collective-permute-start(bf16[128,4096]{1,0:T(8,128)(2,1)} %get-tuple-element.25), channel_id=1, source_target_pairs={{0,1},{1,2},{2,3},{3,0},{4,5},{5,6},{6,7},{7,4},{8,9},{9,10},{10,1... | collective-permute-start | bytes 3145736 | tf_op jit(solution)/shard_map/ppermute | solution.py:12
  146.4 256.2 %copy-start.1 = (f32[1,32,64]{2,1,0:T(8,128)S(1)}, f32[1,32,64]{2,1,0:T(8,128)}, u32[]{:S(2)}) copy-start(f32[1,32,64]{2,1,0:T(8,128)} %param.14) | copy-start | bytes 24580
Sparse Core Ops, SparseCore 0:
  143.4 203.3 all-reduce.3
where the time goes:
time: 410 us; the launch traced here: 409 us
  blocking collectives  328 us (80%)
  matrix products  25.3 us (6%)
  local copies, waits for them, and re-layouts  24.3 us (6%)
  between operations  15.5 us (4%)
  other arithmetic  12.7 us (3%)
    psum x1, blocking collectives, local(): grad_g, grad_b = lax.psum((grad_g, grad_b), 'dp')  248 us
    all_gather x1, blocking collectives, local(): lax.all_gather(token_ids[0], 'dp', axis=0, tiled=True)  42.7 us
    all_gather x1, blocking collectives, local(): lax.all_gather(segment_ids[0], 'dp', axis=0, tiled=True)  37.3 us
  transfers between devices with their start and end apart: 3, of which 0 were waited for; matrix products, arithmetic and copies ran while one was open for 6% of the time, Pallas kernels for 0%

commit v1 on v0

--- a/solution.py
+++ b/solution.py
@@ -58,7 +58,9 @@
 def local(token_ids, segment_ids, row_order, embed_table, norm_gain, position_bias, returned_grad):
     all_ids, all_segs = (
         lax.all_gather(token_ids[0], "dp", axis=0, tiled=True),
-        lax.all_gather(segment_ids[0], "dp", axis=0, tiled=True),
+        jnp.concatenate(
+            lax.all_to_all(jnp.stack([segment_ids[0]] * lax.axis_size("dp")), "dp", 0, 0), axis=0
+        ),
     )
     order = row_order[0]
     packed = jnp.take(all_ids, order, axis=0)

time: 410 us -> 384 us (0.937)
  blocking collectives: 328 us -> 288 us
  starting transfers between devices: 3.43 us -> 15.4 us
    all_gather x1 -> x0, blocking collectives: 37.3 us -> none  [local(): lax.all_gather(segment_ids[0], 'dp', axis=0, tiled=True)]
    all_to_all x0 -> x1, starting transfers between devices: none -> 11.9 us  [local(): lax.all_to_all(jnp.stack([segment_ids[0]] * lax.axis_size('dp')), 'dp', 0...]
  transfers between devices with their start and end apart: 3 -> 4, of which waited for: 0 -> 0; matrix products, arithmetic and copies ran while one was open for 6% -> 6% of each run, Pallas kernels for 0% -> 0%
where the time goes in v1:
time: 384 us; the launch traced here: 383 us
  blocking collectives  288 us (75%)
  local copies, waits for them, and re-layouts  25.6 us (7%)
  matrix products  25.3 us (7%)
  between operations  15.5 us (4%)
  starting transfers between devices  15.4 us (4%)
  other arithmetic  12.7 us (3%)
    psum x1, blocking collectives, local(): grad_g, grad_b = lax.psum((grad_g, grad_b), 'dp')  247 us
    all_gather x1, blocking collectives, local(): lax.all_gather(token_ids[0], 'dp', axis=0, tiled=True)  41 us
    all_to_all x1, starting transfers between devices, local(): lax.all_to_all(jnp.stack([segment_ids[0]] * lax.axis_size('dp')), 'dp', 0...  11.9 us
  transfers between devices with their start and end apart: 4, of which 0 were waited for; matrix products, arithmetic and copies ran while one was open for 6% of the time, Pallas kernels for 0%

profile of v1, /device:TPU:24, one launch (start us, length us, event | category | flops | bytes accessed | tf_op | source)
XLA Modules:
  0.0 382.9 jit_solution(3658364714003314033)
XLA Ops:
  7.2 0.0 copy-start
  7.2 0.0 copy-start.7
  7.2 1.3 stack.3
  8.5 11.9 %all-to-all-start = ((s32[64,1,128]{2,1,0:T(1,128)}), s32[64,1,128]{2,1,0:T(1,128)S(1)}, u32[]{:S(2)}, u32[]{:S(2)}) async-start(s32[64,1,128]{2,1,0:T(1,128)} %stack.3), calls=%async_computation | async-start | bytes 65536 | tf_op jit(solution)/shard_map/all_to_all | solution.py:62
  20.4 0.0 all-reduce.4.cloned.1.call-start
  20.5 0.8 collective-permute-start.1
  21.3 0.1 select_add_fusion
  22.0 41.0 %all-gather = s32[64,1,128]{2,1,0:T(1,128)S(1)} all-gather(s32[1,1,128]{2,1,0:T(1,128)} %param.9), channel_id=2, replica_groups=mesh['dp'=64,'section'=4] {'dp'}, dimensions={0}, use_global_device_ids=true | all-gather | bytes 33280 | tf_op jit(solution)/shard_map/all_gather | solution.py:60
  63.0 3.0 multiply_reduce_fusion.2
  66.1 0.0 copy-done.7
  66.1 1.3 multiply_convert_fusion
  67.4 0.0 copy-done
  67.4 2.7 fusion.17
  70.0 1.6 copy.37
  71.7 5.4 %copy.38 = f32[128,128,64]{0,1,2:T(8,128)} copy(f32[128,128,64]{1,2,0:T(8,128)} %fusion.17) | data formatting | bytes 8388608 | tf_op jit(solution)/shard_map/jvp(qkb,bh->hqk)/dot_general | solution.py:50
  77.1 0.0 all-to-all-done
  77.1 0.1 broadcast_compare_fusion.1
  77.2 3.3 fusion.47
  80.4 0.0 copy-start.2
  80.5 1.9 copy-done.2
  82.4 0.9 fusion.13
  83.3 0.0 collective-permute-done.1
  83.3 2.3 copy.41
  85.6 0.0 copy-start.3
  85.6 4.1 %fusion.6 = (f32[64,128]{1,0:T(8,128)S(1)}, bf16[64,128,128]{2,1,0:T(8,128)(2,1)S(1)}) fusion(f32[64,128,128]{1,2,0:T(8,128)} %copy-done.2, f32[64,128]{1,0:T(8,128)S(1)} %multiply_divide_fusion, f32[64,128]{1,0:T(8,128)S(1)} %get-tuple-element.28, bf16[128,64,64]{0,2,1:T(8,128)(2,1)S(1)} %bitcast.105, bf16[64,64,128]{2,1,0:T(8,128)(2,1)} %bitcast.109), kind=kOutput, calls=%fused_computation.9 | convolution fusion | flops 140500992 | bytes 8486912 | tf_op jit(solution)/shard_map/transpose(jvp(vmap(hqk,khd->qhd)))/dot_general | solution.py:35
  89.7 0.0 copy-done.3
  89.7 2.6 convert_reduce_fusion
  92.3 2.2 add_select_fusion
  94.4 0.0 copy-start.4
  94.5 1.5 fusion.11
  96.0 0.7 fusion.9
  96.7 0.0 copy-done.4
  96.7 0.0 copy-start.6
  96.7 2.0 fusion.50
  98.7 0.0 copy-done.6
  98.7 1.5 fusion.15
  100.2 1.5 bitcast_convert_fusion
  101.8 2.9 copy.45
  104.7 2.9 copy.40
  107.6 0.0 copy-start.5
  107.6 4.0 %multiply_reduce_fusion = (f32[4096]{0:T(1024)S(1)}, f32[128]{0:T(128)S(1)}, bf16[128,4096]{1,0:T(8,128)(2,1)}) fusion(f32[128,4096]{1,0:T(8,128)} %copy.45, f32[128,4096]{1,0:T(8,128)S(1)} %get-tuple-element.27, f32[128]{0:T(128)S(1)} %fusion.42, f32[4096]{0:T(1024)S(1)} %bitcast.114, f32[128,4096]{1,0:T(8,128)} %copy.40), kind=kLoop, calls=%fused_computation.27 | loop fusion | flops 4190080 | bytes 7373824 | tf_op jit(solution)/shard_map/transpose(jvp())/reduce_sum | solution.py:46
  111.6 0.0 copy-done.5
  111.6 5.9 %fusion.21 = f32[512,4096]{1,0:T(8,128)} fusion(f32[128,4096]{1,0:T(8,128)S(1)} %get-tuple-element.27, bf16[128,4096]{1,0:T(8,128)(2,1)} %collective-permute-done.1, f32[128,4096]{1,0:T(8,128)S(1)} %copy-done.5, f32[128]{0:T(128)S(1)} %multiply_multiply_fusion, f32[4096]{0:T(1024)S(1)} %bitcast.115, f32[128]{0:T(128)S(1)} %fusion.42, s32[128]{0:T(128)S(1)} %fusion.40), kind=kOutput, calls=%fused_computation.40 | convolution fusion | flops 541130752 | bytes 13649408 | tf_op jit(solution)/shard_map/dot_general | solution.py:84
  117.5 0.0 copy-start.8
  117.5 0.0 all-reduce.4.cloned.1.call-update
  117.5 2.6 collective-permute-start
  120.1 0.0 copy-done.8
  120.1 0.6 dynamic-slice.7
  120.7 0.0 copy-start.1
  121.3 4.1 %copy.47 = bf16[64,128,128]{2,0,1:T(8,128)(2,1)S(1)} copy(f32[64,128,128]{1,2,0:T(8,128)} %copy-done.4) | data formatting | bytes 6291456 | tf_op jit(solution)/shard_map/transpose(jvp(vmap(jit(_where))))/select_n | solution.py:31
  125.4 0.7 fusion.20
  126.1 247.4 %all-reduce.1 = (f32[1,4096]{1,0:T(1,128)}, f32[1,32,64]{2,1,0:T(8,128)}) all-reduce(f32[1,4096]{1,0:T(1,128)S(1)} %bitcast.116, f32[1,32,64]{2,1,0:T(8,128)S(1)} %fusion.20), channel_id=1, replica_groups=mesh['dp'=64,'section'=4] {'dp'}, use_global_device_ids=true, to_apply=%region_9.11 | all-reduce | flops 6144 | bytes 49152 | tf_op jit(solution)/shard_map/psum | solution.py:88
  373.5 0.0 collective-permute-done
  373.5 0.0 all-reduce.4.cloned.1.call-done
  373.5 1.6 dynamic-slice_bitcast_fusion
  375.1 1.0 copy.55
  376.0 0.0 copy-done.1
  (7 shorter events, 0.1 us)
Async XLA Ops:
  7.2 60.2 %copy-start = (f32[1,32,64]{2,1,0:T(8,128)S(1)}, f32[1,32,64]{2,1,0:T(8,128)}, u32[]{:S(2)}) copy-start(f32[1,32,64]{2,1,0:T(8,128)} %param.14) | copy-start | bytes 24580
  7.2 58.9 %copy-start.7 = (f32[1,4096]{1,0:T(1,128)S(1)}, f32[1,4096]{1,0:T(1,128)}, u32[]{:S(2)}) copy-start(f32[1,4096]{1,0:T(1,128)} %param.13) | copy-start | bytes 49156
  8.5 68.6 %all-to-all-start = ((s32[64,1,128]{2,1,0:T(1,128)}), s32[64,1,128]{2,1,0:T(1,128)S(1)}, u32[]{:S(2)}, u32[]{:S(2)}) async-start(s32[64,1,128]{2,1,0:T(1,128)} %stack.3), calls=%async_computation | async-start | bytes 65536 | tf_op jit(solution)/shard_map/all_to_all | solution.py:62
  20.4 353.1 %all-reduce.4.cloned.1.call-start = ((), (), s32[]{:S(2)}) async-start(), calls=%async_computation.1 | async-start | bytes 16777216
  20.5 62.9 %collective-permute-start.1 = (bf16[128,4096]{1,0:T(8,128)(2,1)}, bf16[128,4096]{1,0:T(8,128)(2,1)}, u32[]{:S(2)}, u32[]{:S(2)}) collective-permute-start(bf16[128,4096]{1,0:T(8,128)(2,1)} %bitcast.120), channel_id=1, source_target_pairs={{0,3},{1,0},{2,1},{3,2},{4,7},{5,4},{6,5},{7,6},{8,11},{9,8},{10,9... | collective-permute-start | bytes 3145736 | tf_op jit(solution)/shard_map/ppermute | solution.py:12
  80.4 1.9 copy-start.2
  85.6 4.1 %copy-start.3 = (f32[64,128,128]{1,2,0:T(8,128)S(1)}, f32[64,128,128]{1,2,0:T(8,128)}, u32[]{:S(2)}) copy-start(f32[64,128,128]{1,2,0:T(8,128)} %copy-done.2) | copy-start | bytes 12582916
  94.4 2.2 copy-start.4
  96.7 2.0 copy-start.6
  107.6 4.0 %copy-start.5 = (f32[128,4096]{1,0:T(8,128)S(1)}, f32[128,4096]{1,0:T(8,128)}, u32[]{:S(2)}) copy-start(f32[128,4096]{1,0:T(8,128)} %copy.45) | copy-start | bytes 6291460
  117.5 2.6 copy-start.8
  117.5 256.0 %collective-permute-start = (bf16[128,4096]{1,0:T(8,128)(2,1)}, bf16[128,4096]{1,0:T(8,128)(2,1)S(1)}, u32[]{:S(2)}, u32[]{:S(2)}) collective-permute-start(bf16[128,4096]{1,0:T(8,128)(2,1)} %get-tuple-element.25), channel_id=1, source_target_pairs={{0,1},{1,2},{2,3},{3,0},{4,5},{5,6},{6,7},{7,4},{8,9},{9,10},{10,1... | collective-permute-start | bytes 3145736 | tf_op jit(solution)/shard_map/ppermute | solution.py:12
  120.7 255.4 %copy-start.1 = (f32[1,32,64]{2,1,0:T(8,128)S(1)}, f32[1,32,64]{2,1,0:T(8,128)}, u32[]{:S(2)}) copy-start(f32[1,32,64]{2,1,0:T(8,128)} %param.14) | copy-start | bytes 24580
Sparse Core Ops, SparseCore 0:
  117.6 203.1 all-reduce.3
